TPU v7x, 32 devices: a whole 2x2x4 slice. The times are simulated.
32 devices in a mesh: group: 4 (over y, core), expert: 8 (over z, x).
Axes of the slice: x: 2, y: 2, z: 4, core: 2. Of those that a mesh axis runs over, the one named last changes fastest.
Arguments:
- tokens: bfloat16 [4096, 4096], P(('group', 'expert')), may hold values from -8 to 8
- router_weight: bfloat16 [4096, 128], replicated, may hold values from -4 to 4
- expert_dest: int32 [4096, 8], P(('group', 'expert')), may hold values from 0 to 127, all different within a row; in each aligned block of 128 rows (0 to 127, 128 to 255, ...) at most 9 rows name the same one
- group_capacity: int32 [4], replicated, may hold values from 4096 to 16383
- expert_capacity: int32 [128], replicated, may hold values from 128 to 511
- w_gate: bfloat16 [128, 4096, 768], P(('group', 'expert')), may hold values from -0.09375 to 0.09375
- w_up: bfloat16 [128, 4096, 768], P(('group', 'expert')), may hold values from -0.09375 to 0.09375
- w_down: bfloat16 [128, 768, 4096], P(('group', 'expert')), may hold values from -0.21875 to 0.21875
Outputs:
- mixed: bfloat16 [4096, 4096], P(('group', 'expert'))
- gating: float32 [4096, 8], P(('group', 'expert'))
Inputs may be any that keep to these rules, and one draw needn't show every extreme that they name: `expert_dest`: each token names 8 different experts; among the tokens of one device no expert is named more than 9 times, and that bound is reached.
All inputs are finite; a program needn't handle non-finite values.
Results may differ from a plain program's by a relative error of at most 0.0058.
Values may be sent and summed in bfloat16 or wider, within the bound.
No kernel may reach another device: no remote copies, remote signals or barrier semaphores. Data moves between devices by JAX's collectives and lax.ppermute only.
A program may use at most 256 MiB of HBM per device.

v0:
```python
import jax
import jax.numpy as jnp
from jax import lax
from jax.sharding import PartitionSpec as P

ITER1 = 10
ITER2 = 10
SLOT_CAP = 9


def balance(scores, gtarget, etarget, n_group, group_total, expert_total):
    rows, experts = scores.shape
    blocks = scores.reshape(rows, n_group, experts // n_group)
    kernel = jnp.sum(blocks, 2)

    def first(step, carry):
        scale_rows, scale_cols = carry
        scale_rows = 1.0 / jnp.sum(kernel * scale_cols[None, :], 1)
        scale_cols = gtarget / group_total(jnp.sum(kernel * scale_rows[:, None], 0))
        return (scale_rows, scale_cols)

    scale_rows, scale_cols = lax.fori_loop(
        0, ITER1, first, (jnp.ones((rows,), jnp.float32), jnp.ones((n_group,), jnp.float32))
    )
    plan = scale_rows[:, None] * kernel * scale_cols[None, :]

    def second(step, carry):
        row_fac, col_fac = carry
        row_fac = plan / jnp.sum(blocks * col_fac[None], 2)
        col_fac = etarget / expert_total(jnp.sum(blocks * row_fac[:, :, None], 0))
        return (row_fac, col_fac)

    row_fac, col_fac = lax.fori_loop(
        0,
        ITER2,
        second,
        (
            jnp.ones((rows, n_group), jnp.float32),
            jnp.ones((n_group, experts // n_group), jnp.float32),
        ),
    )
    return (row_fac[:, :, None] * blocks * col_fac[None]).reshape(rows, experts)


def per_device(
    tokens, router_weight, expert_dest, group_capacity, expert_capacity, w_gate, w_up, w_down
):
    tok_dev, width = tokens.shape
    experts = router_weight.shape[1]
    topk = expert_dest.shape[1]
    n_group = lax.axis_size("group")
    n_lane = lax.axis_size("expert")
    devices = n_group * n_lane
    exp_dev = w_gate.shape[0]
    logits = jnp.dot(tokens, router_weight, preferred_element_type=jnp.float32)
    scores = jnp.exp(logits)
    gcap = group_capacity.astype(jnp.float32)
    gtarget = tok_dev * devices * gcap / jnp.sum(gcap)
    ecap = expert_capacity.astype(jnp.float32).reshape(n_group, experts // n_group)
    etarget = (gtarget / jnp.sum(ecap, 1))[:, None] * ecap
    balanced = balance(
        scores,
        gtarget,
        etarget,
        n_group,
        lambda part: lax.psum(part, ("group", "expert")),
        lambda part: lax.psum(part, ("group", "expert")),
    )
    gating = jnp.take_along_axis(balanced, expert_dest, axis=1) * (experts / topk)
    flat_dest = expert_dest.reshape(-1)
    onehot = (flat_dest[:, None] == jnp.arange(experts, dtype=jnp.int32)[None, :]).astype(jnp.int32)
    position = jnp.sum(jnp.cumsum(onehot, 0) * onehot, 1) - 1
    slot = flat_dest * SLOT_CAP + position
    token_of = jnp.arange(tok_dev * topk, dtype=jnp.int32) // topk
    outgoing = jnp.zeros((experts * SLOT_CAP, width), jnp.bfloat16).at[slot].set(tokens[token_of])
    outgoing = outgoing.reshape(devices, exp_dev, SLOT_CAP, width)
    arrived = lax.all_to_all(outgoing, ("group", "expert"), split_axis=0, concat_axis=0, tiled=True)
    gate = jnp.einsum("skcd,kdf->skcf", arrived, w_gate, preferred_element_type=jnp.float32)
    up = jnp.einsum("skcd,kdf->skcf", arrived, w_up, preferred_element_type=jnp.float32)
    hidden = (jax.nn.silu(gate) * up).astype(jnp.bfloat16)
    returned = lax.all_to_all(
        jnp.einsum("skcf,kfd->skcd", hidden, w_down, preferred_element_type=jnp.float32).astype(
            jnp.bfloat16
        ),
        ("group", "expert"),
        split_axis=0,
        concat_axis=0,
        tiled=True,
    )
    expert_rows = returned.reshape(experts * SLOT_CAP, width)[slot]
    weighted = gating.reshape(-1, 1) * expert_rows.astype(jnp.float32)
    mixed = jnp.sum(weighted.reshape(tok_dev, topk, width), 1).astype(jnp.bfloat16)
    return (mixed, gating)


def solution(mesh):
    return jax.shard_map(
        per_device,
        mesh=mesh,
        in_specs=(
            P(("group", "expert"), None),
            P(),
            P(("group", "expert"), None),
            P(),
            P(),
            P(("group", "expert"), None, None),
            P(("group", "expert"), None, None),
            P(("group", "expert"), None, None),
        ),
        out_specs=(P(("group", "expert"), None), P(("group", "expert"), None)),
        check_vma=False,
    )
```

profile of v0, /device:TPU:0, one launch (start us, length us, event | category | flops | bytes accessed | tf_op | source)
XLA Modules:
  0.0 1429.2 jit_solution(244274422835837965)
XLA Ops:
  57.3 214.5 %all_to_all.10 = bf16[32,4,9,4096]{3,1,2,0:T(4,128)(2,1)} all-to-all(bf16[32,4,9,4096]{3,1,2,0:T(4,128)(2,1)S(1)} %copy.77), channel_id=1, replica_groups=mesh['group'=4,'expert'=8] {'group','expert'}, dimensions={0} | all-to-all | bytes 18874368 | tf_op jit(solution)/shard_map/all_to_all | solution.py:77
  300.6 29.6 %fusion.13 = bf16[32,4,9,768]{3,0,2,1:T(8,128)(2,1)} fusion(f32[4,32,9,768]{3,1,2,0:T(8,128)} %fusion.2, bf16[4,4096,768]{2,1,0:T(8,128)(2,1)} %param.17, bf16[32,4,9,4096]{3,1,2,0:T(4,128)(2,1)} %all_to_all.10), kind=kOutput, calls=%fused_computation.25 | convolution fusion | flops 7253065728 | bytes 39911424 | tf_op jit(solution)/shard_map/skcd,kdf->skcf/dot_general | solution.py:78
  365.1 589.8 %while.26 = (s32[]{:T(128)}, f32[128]{0:T(128)}, f32[4]{0:T(128)S(1)}, f32[128,4]{0,1:T(4,128)S(1)}, f32[4]{0:T(128)S(1)}, /*index=5*/s32[]{:T(128)}, s32[]{:T(128)}) while((s32[]{:T(128)}, f32[128]{0:T(128)}, f32[4]{0:T(128)S(1)}, f32[128,4]{0,1:T(4,128)S(1)}, f32[4]{0:T(128)S(1)}, /*index=5*/s32[]{:T(128)}, s32[]{:T(128)}) %tuple.55), condition=%wide.region_6.7_spmd.clone, body=%wide.region_2.6_spmd.clone.sunk | while | flops 2059 | bytes 8459 | solution.py:22
  365.3 229.2 %psum.18 = f32[4]{0:T(128)S(1)} all-reduce(f32[4]{0:T(128)S(1)} %multiply_reduce_fusion.9), channel_id=1, replica_groups=mesh['group'=4,'expert'=8] {'group','expert'}, use_global_device_ids=true, to_apply=%region_5.0 | all-reduce | flops 4 | bytes 32 | tf_op jit(solution)/shard_map/while/body/eval_jaxpr/psum | solution.py:66
  594.8 38.4 %psum.18 = f32[4]{0:T(128)S(1)} all-reduce(f32[4]{0:T(128)S(1)} %multiply_reduce_fusion.9), channel_id=1, replica_groups=mesh['group'=4,'expert'=8] {'group','expert'}, use_global_device_ids=true, to_apply=%region_5.0 | all-reduce | flops 4 | bytes 32 | tf_op jit(solution)/shard_map/while/body/eval_jaxpr/psum | solution.py:66
  633.4 41.5 %psum.18 = f32[4]{0:T(128)S(1)} all-reduce(f32[4]{0:T(128)S(1)} %multiply_reduce_fusion.9), channel_id=1, replica_groups=mesh['group'=4,'expert'=8] {'group','expert'}, use_global_device_ids=true, to_apply=%region_5.0 | all-reduce | flops 4 | bytes 32 | tf_op jit(solution)/shard_map/while/body/eval_jaxpr/psum | solution.py:66
  675.2 38.4 %psum.18 = f32[4]{0:T(128)S(1)} all-reduce(f32[4]{0:T(128)S(1)} %multiply_reduce_fusion.9), channel_id=1, replica_groups=mesh['group'=4,'expert'=8] {'group','expert'}, use_global_device_ids=true, to_apply=%region_5.0 | all-reduce | flops 4 | bytes 32 | tf_op jit(solution)/shard_map/while/body/eval_jaxpr/psum | solution.py:66
  713.8 41.5 %psum.18 = f32[4]{0:T(128)S(1)} all-reduce(f32[4]{0:T(128)S(1)} %multiply_reduce_fusion.9), channel_id=1, replica_groups=mesh['group'=4,'expert'=8] {'group','expert'}, use_global_device_ids=true, to_apply=%region_5.0 | all-reduce | flops 4 | bytes 32 | tf_op jit(solution)/shard_map/while/body/eval_jaxpr/psum | solution.py:66
  755.6 38.4 %psum.18 = f32[4]{0:T(128)S(1)} all-reduce(f32[4]{0:T(128)S(1)} %multiply_reduce_fusion.9), channel_id=1, replica_groups=mesh['group'=4,'expert'=8] {'group','expert'}, use_global_device_ids=true, to_apply=%region_5.0 | all-reduce | flops 4 | bytes 32 | tf_op jit(solution)/shard_map/while/body/eval_jaxpr/psum | solution.py:66
  794.2 41.5 %psum.18 = f32[4]{0:T(128)S(1)} all-reduce(f32[4]{0:T(128)S(1)} %multiply_reduce_fusion.9), channel_id=1, replica_groups=mesh['group'=4,'expert'=8] {'group','expert'}, use_global_device_ids=true, to_apply=%region_5.0 | all-reduce | flops 4 | bytes 32 | tf_op jit(solution)/shard_map/while/body/eval_jaxpr/psum | solution.py:66
  835.9 38.5 %psum.18 = f32[4]{0:T(128)S(1)} all-reduce(f32[4]{0:T(128)S(1)} %multiply_reduce_fusion.9), channel_id=1, replica_groups=mesh['group'=4,'expert'=8] {'group','expert'}, use_global_device_ids=true, to_apply=%region_5.0 | all-reduce | flops 4 | bytes 32 | tf_op jit(solution)/shard_map/while/body/eval_jaxpr/psum | solution.py:66
  874.7 41.4 %psum.18 = f32[4]{0:T(128)S(1)} all-reduce(f32[4]{0:T(128)S(1)} %multiply_reduce_fusion.9), channel_id=1, replica_groups=mesh['group'=4,'expert'=8] {'group','expert'}, use_global_device_ids=true, to_apply=%region_5.0 | all-reduce | flops 4 | bytes 32 | tf_op jit(solution)/shard_map/while/body/eval_jaxpr/psum | solution.py:66
  916.3 38.6 %psum.18 = f32[4]{0:T(128)S(1)} all-reduce(f32[4]{0:T(128)S(1)} %multiply_reduce_fusion.9), channel_id=1, replica_groups=mesh['group'=4,'expert'=8] {'group','expert'}, use_global_device_ids=true, to_apply=%region_5.0 | all-reduce | flops 4 | bytes 32 | tf_op jit(solution)/shard_map/while/body/eval_jaxpr/psum | solution.py:66
  955.9 405.0 %while.27 = (s32[]{:T(128)}, f32[128,4]{1,0:T(8,128)}, f32[4,32]{1,0:T(4,128)S(1)}, f32[128,4,32]{2,1,0:T(4,128)S(1)}, f32[128,4]{1,0:T(8,128)S(1)}, /*index=5*/f32[4,32]{1,0:T(4,128)S(1)}, s32[]{:T(128)}, s32[]{:T(128)}) while((s32[]{:T(128)}, f32[128,4]{1,0:T(8,128)}, f32[4,32]{1,0:T(4,128)S(1)}, f32[128,4,32]{2,1,0:T(4,128)S(1)}, ...), condition=%wide.region_12.0_spmd.clone, body=%wide.region_8.0_spmd.clone.sunk | while | flops 65795 | bytes 154243 | solution.py:33
  956.3 41.3 %psum.19 = f32[4,32]{1,0:T(4,128)S(1)} all-reduce(f32[4,32]{1,0:T(4,128)S(1)} %multiply_reduce_fusion.11), channel_id=1, replica_groups=mesh['group'=4,'expert'=8] {'group','expert'}, use_global_device_ids=true, to_apply=%region_11.0 | all-reduce | flops 128 | bytes 1024 | tf_op jit(solution)/shard_map/while/body/eval_jaxpr/psum | solution.py:67
  998.1 38.7 %psum.19 = f32[4,32]{1,0:T(4,128)S(1)} all-reduce(f32[4,32]{1,0:T(4,128)S(1)} %multiply_reduce_fusion.11), channel_id=1, replica_groups=mesh['group'=4,'expert'=8] {'group','expert'}, use_global_device_ids=true, to_apply=%region_11.0 | all-reduce | flops 128 | bytes 1024 | tf_op jit(solution)/shard_map/while/body/eval_jaxpr/psum | solution.py:67
  1037.3 41.2 %psum.19 = f32[4,32]{1,0:T(4,128)S(1)} all-reduce(f32[4,32]{1,0:T(4,128)S(1)} %multiply_reduce_fusion.11), channel_id=1, replica_groups=mesh['group'=4,'expert'=8] {'group','expert'}, use_global_device_ids=true, to_apply=%region_11.0 | all-reduce | flops 128 | bytes 1024 | tf_op jit(solution)/shard_map/while/body/eval_jaxpr/psum | solution.py:67
  1079.0 38.8 %psum.19 = f32[4,32]{1,0:T(4,128)S(1)} all-reduce(f32[4,32]{1,0:T(4,128)S(1)} %multiply_reduce_fusion.11), channel_id=1, replica_groups=mesh['group'=4,'expert'=8] {'group','expert'}, use_global_device_ids=true, to_apply=%region_11.0 | all-reduce | flops 128 | bytes 1024 | tf_op jit(solution)/shard_map/while/body/eval_jaxpr/psum | solution.py:67
  1118.3 41.2 %psum.19 = f32[4,32]{1,0:T(4,128)S(1)} all-reduce(f32[4,32]{1,0:T(4,128)S(1)} %multiply_reduce_fusion.11), channel_id=1, replica_groups=mesh['group'=4,'expert'=8] {'group','expert'}, use_global_device_ids=true, to_apply=%region_11.0 | all-reduce | flops 128 | bytes 1024 | tf_op jit(solution)/shard_map/while/body/eval_jaxpr/psum | solution.py:67
  1160.0 38.8 %psum.19 = f32[4,32]{1,0:T(4,128)S(1)} all-reduce(f32[4,32]{1,0:T(4,128)S(1)} %multiply_reduce_fusion.11), channel_id=1, replica_groups=mesh['group'=4,'expert'=8] {'group','expert'}, use_global_device_ids=true, to_apply=%region_11.0 | all-reduce | flops 128 | bytes 1024 | tf_op jit(solution)/shard_map/while/body/eval_jaxpr/psum | solution.py:67
  1199.3 41.2 %psum.19 = f32[4,32]{1,0:T(4,128)S(1)} all-reduce(f32[4,32]{1,0:T(4,128)S(1)} %multiply_reduce_fusion.11), channel_id=1, replica_groups=mesh['group'=4,'expert'=8] {'group','expert'}, use_global_device_ids=true, to_apply=%region_11.0 | all-reduce | flops 128 | bytes 1024 | tf_op jit(solution)/shard_map/while/body/eval_jaxpr/psum | solution.py:67
  1241.0 38.8 %psum.19 = f32[4,32]{1,0:T(4,128)S(1)} all-reduce(f32[4,32]{1,0:T(4,128)S(1)} %multiply_reduce_fusion.11), channel_id=1, replica_groups=mesh['group'=4,'expert'=8] {'group','expert'}, use_global_device_ids=true, to_apply=%region_11.0 | all-reduce | flops 128 | bytes 1024 | tf_op jit(solution)/shard_map/while/body/eval_jaxpr/psum | solution.py:67
  1280.3 41.2 %psum.19 = f32[4,32]{1,0:T(4,128)S(1)} all-reduce(f32[4,32]{1,0:T(4,128)S(1)} %multiply_reduce_fusion.11), channel_id=1, replica_groups=mesh['group'=4,'expert'=8] {'group','expert'}, use_global_device_ids=true, to_apply=%region_11.0 | all-reduce | flops 128 | bytes 1024 | tf_op jit(solution)/shard_map/while/body/eval_jaxpr/psum | solution.py:67
  1322.0 38.9 %psum.19 = f32[4,32]{1,0:T(4,128)S(1)} all-reduce(f32[4,32]{1,0:T(4,128)S(1)} %multiply_reduce_fusion.11), channel_id=1, replica_groups=mesh['group'=4,'expert'=8] {'group','expert'}, use_global_device_ids=true, to_apply=%region_11.0 | all-reduce | flops 128 | bytes 1024 | tf_op jit(solution)/shard_map/while/body/eval_jaxpr/psum | solution.py:67
  (209 shorter events, 195.9 us)
Async XLA Ops:
  358.9 4.8 copy-start.6
  358.9 1002.9 %copy-start.3 = (s32[128,8]{0,1:T(8,128)S(1)}, s32[128,8]{0,1:T(8,128)}, u32[]{:S(2)}) copy-start(s32[128,8]{0,1:T(8,128)} %param.14) | copy-start | bytes 12292
  358.9 1010.5 %all-to-all-start.1 = ((bf16[32,4,9,4096]{3,1,2,0:T(4,128)(2,1)}), bf16[32,4,9,4096]{3,1,2,0:T(4,128)(2,1)}, u32[]{:S(2)}, u32[]{:S(2)}) async-start(bf16[32,4,9,4096]{3,1,2,0:T(4,128)(2,1)} %copy.80), calls=%async_computation.1 | async-start | bytes 18874368 | tf_op jit(solution)/shard_map/all_to_all | solution.py:81
  365.2 229.4 %copy-start.4 = (f32[128]{0:T(128)}, f32[128]{0:T(128)S(1)}, u32[]{:S(2)}) copy-start(f32[128]{0:T(128)S(1)} %broadcast_divide_fusion.2) | copy-start | bytes 1540 | tf_op jit(solution)/shard_map/while
  594.7 38.5 %copy-start.4 = (f32[128]{0:T(128)}, f32[128]{0:T(128)S(1)}, u32[]{:S(2)}) copy-start(f32[128]{0:T(128)S(1)} %broadcast_divide_fusion.2) | copy-start | bytes 1540 | tf_op jit(solution)/shard_map/while
  633.3 41.6 %copy-start.4 = (f32[128]{0:T(128)}, f32[128]{0:T(128)S(1)}, u32[]{:S(2)}) copy-start(f32[128]{0:T(128)S(1)} %broadcast_divide_fusion.2) | copy-start | bytes 1540 | tf_op jit(solution)/shard_map/while
  675.1 38.5 %copy-start.4 = (f32[128]{0:T(128)}, f32[128]{0:T(128)S(1)}, u32[]{:S(2)}) copy-start(f32[128]{0:T(128)S(1)} %broadcast_divide_fusion.2) | copy-start | bytes 1540 | tf_op jit(solution)/shard_map/while
  713.7 41.6 %copy-start.4 = (f32[128]{0:T(128)}, f32[128]{0:T(128)S(1)}, u32[]{:S(2)}) copy-start(f32[128]{0:T(128)S(1)} %broadcast_divide_fusion.2) | copy-start | bytes 1540 | tf_op jit(solution)/shard_map/while
  755.4 38.6 %copy-start.4 = (f32[128]{0:T(128)}, f32[128]{0:T(128)S(1)}, u32[]{:S(2)}) copy-start(f32[128]{0:T(128)S(1)} %broadcast_divide_fusion.2) | copy-start | bytes 1540 | tf_op jit(solution)/shard_map/while
  794.1 41.6 %copy-start.4 = (f32[128]{0:T(128)}, f32[128]{0:T(128)S(1)}, u32[]{:S(2)}) copy-start(f32[128]{0:T(128)S(1)} %broadcast_divide_fusion.2) | copy-start | bytes 1540 | tf_op jit(solution)/shard_map/while
  835.8 38.6 %copy-start.4 = (f32[128]{0:T(128)}, f32[128]{0:T(128)S(1)}, u32[]{:S(2)}) copy-start(f32[128]{0:T(128)S(1)} %broadcast_divide_fusion.2) | copy-start | bytes 1540 | tf_op jit(solution)/shard_map/while
  874.6 41.5 %copy-start.4 = (f32[128]{0:T(128)}, f32[128]{0:T(128)S(1)}, u32[]{:S(2)}) copy-start(f32[128]{0:T(128)S(1)} %broadcast_divide_fusion.2) | copy-start | bytes 1540 | tf_op jit(solution)/shard_map/while
  916.2 38.7 %copy-start.4 = (f32[128]{0:T(128)}, f32[128]{0:T(128)S(1)}, u32[]{:S(2)}) copy-start(f32[128]{0:T(128)S(1)} %broadcast_divide_fusion.2) | copy-start | bytes 1540 | tf_op jit(solution)/shard_map/while
  956.1 41.6 %copy-start.1 = (f32[128,4]{1,0:T(8,128)}, f32[128,4]{1,0:T(8,128)S(1)}, u32[]{:S(2)}) copy-start(f32[128,4]{1,0:T(8,128)S(1)} %div.73) | copy-start | bytes 6148 | tf_op jit(solution)/shard_map/while
  997.9 38.9 %copy-start.1 = (f32[128,4]{1,0:T(8,128)}, f32[128,4]{1,0:T(8,128)S(1)}, u32[]{:S(2)}) copy-start(f32[128,4]{1,0:T(8,128)S(1)} %div.73) | copy-start | bytes 6148 | tf_op jit(solution)/shard_map/while
  1037.1 41.5 %copy-start.1 = (f32[128,4]{1,0:T(8,128)}, f32[128,4]{1,0:T(8,128)S(1)}, u32[]{:S(2)}) copy-start(f32[128,4]{1,0:T(8,128)S(1)} %div.73) | copy-start | bytes 6148 | tf_op jit(solution)/shard_map/while
  1078.8 39.0 %copy-start.1 = (f32[128,4]{1,0:T(8,128)}, f32[128,4]{1,0:T(8,128)S(1)}, u32[]{:S(2)}) copy-start(f32[128,4]{1,0:T(8,128)S(1)} %div.73) | copy-start | bytes 6148 | tf_op jit(solution)/shard_map/while
  1118.1 41.4 %copy-start.1 = (f32[128,4]{1,0:T(8,128)}, f32[128,4]{1,0:T(8,128)S(1)}, u32[]{:S(2)}) copy-start(f32[128,4]{1,0:T(8,128)S(1)} %div.73) | copy-start | bytes 6148 | tf_op jit(solution)/shard_map/while
  1159.8 39.0 %copy-start.1 = (f32[128,4]{1,0:T(8,128)}, f32[128,4]{1,0:T(8,128)S(1)}, u32[]{:S(2)}) copy-start(f32[128,4]{1,0:T(8,128)S(1)} %div.73) | copy-start | bytes 6148 | tf_op jit(solution)/shard_map/while
  1199.1 41.4 %copy-start.1 = (f32[128,4]{1,0:T(8,128)}, f32[128,4]{1,0:T(8,128)S(1)}, u32[]{:S(2)}) copy-start(f32[128,4]{1,0:T(8,128)S(1)} %div.73) | copy-start | bytes 6148 | tf_op jit(solution)/shard_map/while
  1240.8 39.0 %copy-start.1 = (f32[128,4]{1,0:T(8,128)}, f32[128,4]{1,0:T(8,128)S(1)}, u32[]{:S(2)}) copy-start(f32[128,4]{1,0:T(8,128)S(1)} %div.73) | copy-start | bytes 6148 | tf_op jit(solution)/shard_map/while
  1280.0 41.4 %copy-start.1 = (f32[128,4]{1,0:T(8,128)}, f32[128,4]{1,0:T(8,128)S(1)}, u32[]{:S(2)}) copy-start(f32[128,4]{1,0:T(8,128)S(1)} %div.73) | copy-start | bytes 6148 | tf_op jit(solution)/shard_map/while
  1321.7 39.1 %copy-start.1 = (f32[128,4]{1,0:T(8,128)}, f32[128,4]{1,0:T(8,128)S(1)}, u32[]{:S(2)}) copy-start(f32[128,4]{1,0:T(8,128)S(1)} %div.73) | copy-start | bytes 6148 | tf_op jit(solution)/shard_map/while
  1369.3 10.9 copy-start.5
  (3 other events, 11.4 us)
where the time goes:
time: 1440 us; the launch traced here: 1430 us
  blocking collectives  1200 us (83%)
  local copies, waits for them, and re-layouts  124 us (9%)
  matrix products  74.2 us (5%)
  other arithmetic  23.3 us (2%)
    psum x20, blocking collectives, per_device(): lax.psum(part, ('group', 'expert'))  987 us
    all_to_all x1, blocking collectives, per_device(): lax.all_to_all(outgoing, ('group', 'expert'), split_axis=0, concat_axis=0...  214 us
    dot_general x1, matrix products, per_device(): jnp.einsum('skcd,kdf->skcf', arrived, w_gate, preferred_element_type=jnp....  29.6 us
  transfers between devices with their start and end apart: 1, of which 0 were waited for; matrix products, arithmetic and copies ran while one was open for 1% of the time, Pallas kernels for 0%

commit v1 on v0

--- a/solution.py
+++ b/solution.py
@@ -1,3 +1,4 @@
+import functools
 import jax
 import jax.numpy as jnp
 from jax import lax
@@ -6,6 +7,15 @@
 ITER1 = 10
 ITER2 = 10
 SLOT_CAP = 9
+
+
+def _push_clusters(x_part, mesh_name, along_axis):
+    seen_now = lax.psum(x_part, mesh_name)
+    near = lax.psum(seen_now, along_axis)
+    return near
+
+
+shards_drive = functools.partial(_push_clusters, mesh_name="expert", along_axis="group")
 
 
 def balance(scores, gtarget, etarget, n_group, group_total, expert_total):
@@ -64,7 +74,7 @@
         etarget,
         n_group,
         lambda part: lax.psum(part, ("group", "expert")),
-        lambda part: lax.psum(part, ("group", "expert")),
+        lambda part: shards_drive(part),
     )
     gating = jnp.take_along_axis(balanced, expert_dest, axis=1) * (experts / topk)
     flat_dest = expert_dest.reshape(-1)

time: 1440 us -> 1280 us (0.89)
  blocking collectives: 1200 us -> 1040 us
    psum x20 -> x10, blocking collectives: 987 us -> 587 us  [per_device(): lax.psum(part, ('group', 'expert'))]
    psum x0 -> x20, blocking collectives: none -> 240 us  [the longest x10 183 us: _push_clusters(): seen_now = lax.psum(x_part, mesh_name)]
where the time goes in v1:
time: 1280 us; the launch traced here: 1270 us
  blocking collectives  1040 us (81%)
  local copies, waits for them, and re-layouts  124 us (10%)
  matrix products  74.2 us (6%)
  other arithmetic  23.3 us (2%)
    psum x10, blocking collectives, per_device(): lax.psum(part, ('group', 'expert'))  587 us
    all_to_all x1, blocking collectives, per_device(): lax.all_to_all(outgoing, ('group', 'expert'), split_axis=0, concat_axis=0...  214 us
    psum x10, blocking collectives, _push_clusters(): seen_now = lax.psum(x_part, mesh_name)  183 us
    psum x10, blocking collectives, _push_clusters(): near = lax.psum(seen_now, along_axis)  56.9 us
    dot_general x1, matrix products, per_device(): jnp.einsum('skcd,kdf->skcf', arrived, w_gate, preferred_element_type=jnp....  29.6 us
    dot_general x1, matrix products, per_device(): jnp.einsum('skcd,kdf->skcf', arrived, w_up, preferred_element_type=jnp.fl...  28.7 us
    reshape x2, local copies, waits for them, and re-layouts, per_device(): outgoing = outgoing.reshape(devices, exp_dev, SLOT_CAP, width)  27.7 us
  transfers between devices with their start and end apart: 1, of which 0 were waited for; matrix products, arithmetic and copies ran while one was open for 1% of the time, Pallas kernels for 0%

profile of v1, /device:TPU:0, one launch (start us, length us, event | category | flops | bytes accessed | tf_op | source)
XLA Modules:
  0.0 1268.7 jit_solution(469630006628916467)
XLA Ops:
  11.3 18.4 %scatter_custom_fusion = bf16[1152,4096]{1,0:T(8,128)(2,1)} fusion(s32[1024]{0:T(1024)S(1)} %bitcast.66, bf16[1024,4096]{1,0:T(8,128)(2,1)} %gather_fusion, bf16[]{:T(256)} %constant.68.clone.1), kind=kCustom, calls=%fused_computation.22 | custom fusion | bytes 9437696 | tf_op jit(solution)/shard_map/scatter | solution.py:85
  57.3 214.5 %all_to_all.10 = bf16[32,4,9,4096]{3,1,2,0:T(4,128)(2,1)} all-to-all(bf16[32,4,9,4096]{3,1,2,0:T(4,128)(2,1)S(1)} %copy.77), channel_id=1, replica_groups=mesh['group'=4,'expert'=8] {'group','expert'}, dimensions={0} | all-to-all | bytes 18874368 | tf_op jit(solution)/shard_map/all_to_all | solution.py:87
  271.8 28.7 %fusion.2 = f32[4,32,9,768]{3,1,2,0:T(8,128)} fusion(bf16[4,4096,768]{2,1,0:T(8,128)(2,1)} %param.18, bf16[32,4,9,4096]{3,1,2,0:T(4,128)(2,1)} %all_to_all.10), kind=kOutput, calls=%fused_computation.13 | convolution fusion | flops 7247757312 | bytes 38141952 | tf_op jit(solution)/shard_map/skcd,kdf->skcf/dot_general | solution.py:89
  300.6 29.6 %fusion.13 = bf16[32,4,9,768]{3,0,2,1:T(8,128)(2,1)} fusion(f32[4,32,9,768]{3,1,2,0:T(8,128)} %fusion.2, bf16[4,4096,768]{2,1,0:T(8,128)(2,1)} %param.17, bf16[32,4,9,4096]{3,1,2,0:T(4,128)(2,1)} %all_to_all.10), kind=kOutput, calls=%fused_computation.25 | convolution fusion | flops 7253065728 | bytes 39911424 | tf_op jit(solution)/shard_map/skcd,kdf->skcf/dot_general | solution.py:88
  365.1 589.8 %while.26 = (s32[]{:T(128)}, f32[128]{0:T(128)}, f32[4]{0:T(128)S(1)}, f32[128,4]{0,1:T(4,128)S(1)}, f32[4]{0:T(128)S(1)}, /*index=5*/s32[]{:T(128)}, s32[]{:T(128)}) while((s32[]{:T(128)}, f32[128]{0:T(128)}, f32[4]{0:T(128)S(1)}, f32[128,4]{0,1:T(4,128)S(1)}, f32[4]{0:T(128)S(1)}, /*index=5*/s32[]{:T(128)}, s32[]{:T(128)}) %tuple.55), condition=%wide.region_6.7_spmd.clone, body=%wide.region_2.6_spmd.clone.sunk | while | flops 2059 | bytes 8459 | solution.py:32
  365.3 229.2 %psum.27 = f32[4]{0:T(128)S(1)} all-reduce(f32[4]{0:T(128)S(1)} %multiply_reduce_fusion.9), channel_id=1, replica_groups=mesh['group'=4,'expert'=8] {'group','expert'}, use_global_device_ids=true, to_apply=%region_5.0 | all-reduce | flops 4 | bytes 32 | tf_op jit(solution)/shard_map/while/body/eval_jaxpr/psum | solution.py:76
  594.8 38.4 %psum.27 = f32[4]{0:T(128)S(1)} all-reduce(f32[4]{0:T(128)S(1)} %multiply_reduce_fusion.9), channel_id=1, replica_groups=mesh['group'=4,'expert'=8] {'group','expert'}, use_global_device_ids=true, to_apply=%region_5.0 | all-reduce | flops 4 | bytes 32 | tf_op jit(solution)/shard_map/while/body/eval_jaxpr/psum | solution.py:76
  633.4 41.5 %psum.27 = f32[4]{0:T(128)S(1)} all-reduce(f32[4]{0:T(128)S(1)} %multiply_reduce_fusion.9), channel_id=1, replica_groups=mesh['group'=4,'expert'=8] {'group','expert'}, use_global_device_ids=true, to_apply=%region_5.0 | all-reduce | flops 4 | bytes 32 | tf_op jit(solution)/shard_map/while/body/eval_jaxpr/psum | solution.py:76
  675.2 38.4 %psum.27 = f32[4]{0:T(128)S(1)} all-reduce(f32[4]{0:T(128)S(1)} %multiply_reduce_fusion.9), channel_id=1, replica_groups=mesh['group'=4,'expert'=8] {'group','expert'}, use_global_device_ids=true, to_apply=%region_5.0 | all-reduce | flops 4 | bytes 32 | tf_op jit(solution)/shard_map/while/body/eval_jaxpr/psum | solution.py:76
  713.8 41.5 %psum.27 = f32[4]{0:T(128)S(1)} all-reduce(f32[4]{0:T(128)S(1)} %multiply_reduce_fusion.9), channel_id=1, replica_groups=mesh['group'=4,'expert'=8] {'group','expert'}, use_global_device_ids=true, to_apply=%region_5.0 | all-reduce | flops 4 | bytes 32 | tf_op jit(solution)/shard_map/while/body/eval_jaxpr/psum | solution.py:76
  755.6 38.4 %psum.27 = f32[4]{0:T(128)S(1)} all-reduce(f32[4]{0:T(128)S(1)} %multiply_reduce_fusion.9), channel_id=1, replica_groups=mesh['group'=4,'expert'=8] {'group','expert'}, use_global_device_ids=true, to_apply=%region_5.0 | all-reduce | flops 4 | bytes 32 | tf_op jit(solution)/shard_map/while/body/eval_jaxpr/psum | solution.py:76
  794.2 41.5 %psum.27 = f32[4]{0:T(128)S(1)} all-reduce(f32[4]{0:T(128)S(1)} %multiply_reduce_fusion.9), channel_id=1, replica_groups=mesh['group'=4,'expert'=8] {'group','expert'}, use_global_device_ids=true, to_apply=%region_5.0 | all-reduce | flops 4 | bytes 32 | tf_op jit(solution)/shard_map/while/body/eval_jaxpr/psum | solution.py:76
  835.9 38.5 %psum.27 = f32[4]{0:T(128)S(1)} all-reduce(f32[4]{0:T(128)S(1)} %multiply_reduce_fusion.9), channel_id=1, replica_groups=mesh['group'=4,'expert'=8] {'group','expert'}, use_global_device_ids=true, to_apply=%region_5.0 | all-reduce | flops 4 | bytes 32 | tf_op jit(solution)/shard_map/while/body/eval_jaxpr/psum | solution.py:76
  874.7 41.4 %psum.27 = f32[4]{0:T(128)S(1)} all-reduce(f32[4]{0:T(128)S(1)} %multiply_reduce_fusion.9), channel_id=1, replica_groups=mesh['group'=4,'expert'=8] {'group','expert'}, use_global_device_ids=true, to_apply=%region_5.0 | all-reduce | flops 4 | bytes 32 | tf_op jit(solution)/shard_map/while/body/eval_jaxpr/psum | solution.py:76
  916.3 38.6 %psum.27 = f32[4]{0:T(128)S(1)} all-reduce(f32[4]{0:T(128)S(1)} %multiply_reduce_fusion.9), channel_id=1, replica_groups=mesh['group'=4,'expert'=8] {'group','expert'}, use_global_device_ids=true, to_apply=%region_5.0 | all-reduce | flops 4 | bytes 32 | tf_op jit(solution)/shard_map/while/body/eval_jaxpr/psum | solution.py:76
  955.9 244.5 %while.27 = (s32[]{:T(128)}, f32[128,4]{1,0:T(8,128)}, f32[4,32]{1,0:T(4,128)S(1)}, f32[128,4,32]{2,1,0:T(4,128)S(1)}, f32[128,4]{1,0:T(8,128)S(1)}, /*index=5*/f32[4,32]{1,0:T(4,128)S(1)}, s32[]{:T(128)}, s32[]{:T(128)}) while((s32[]{:T(128)}, f32[128,4]{1,0:T(8,128)}, f32[4,32]{1,0:T(4,128)S(1)}, f32[128,4,32]{2,1,0:T(4,128)S(1)}, ...), condition=%wide.region_13.0_spmd.clone, body=%wide.region_8.0_spmd.clone.sunk | while | flops 65923 | bytes 155267 | solution.py:43
  956.3 20.5 %psum.28 = f32[4,32]{1,0:T(4,128)S(1)} all-reduce(f32[4,32]{1,0:T(4,128)S(1)} %multiply_reduce_fusion.11), channel_id=1, replica_groups=mesh['group'=4,'expert'=8] {'expert'}, use_global_device_ids=true, to_apply=%region_11.0 | all-reduce | flops 128 | bytes 1024 | tf_op jit(solution)/shard_map/while/body/eval_jaxpr/psum | solution.py:13
  1006.2 19.1 %psum.28 = f32[4,32]{1,0:T(4,128)S(1)} all-reduce(f32[4,32]{1,0:T(4,128)S(1)} %multiply_reduce_fusion.11), channel_id=1, replica_groups=mesh['group'=4,'expert'=8] {'expert'}, use_global_device_ids=true, to_apply=%region_11.0 | all-reduce | flops 128 | bytes 1024 | tf_op jit(solution)/shard_map/while/body/eval_jaxpr/psum | solution.py:13
  1031.5 17.2 %psum.28 = f32[4,32]{1,0:T(4,128)S(1)} all-reduce(f32[4,32]{1,0:T(4,128)S(1)} %multiply_reduce_fusion.11), channel_id=1, replica_groups=mesh['group'=4,'expert'=8] {'expert'}, use_global_device_ids=true, to_apply=%region_11.0 | all-reduce | flops 128 | bytes 1024 | tf_op jit(solution)/shard_map/while/body/eval_jaxpr/psum | solution.py:13
  1054.8 19.1 %psum.28 = f32[4,32]{1,0:T(4,128)S(1)} all-reduce(f32[4,32]{1,0:T(4,128)S(1)} %multiply_reduce_fusion.11), channel_id=1, replica_groups=mesh['group'=4,'expert'=8] {'expert'}, use_global_device_ids=true, to_apply=%region_11.0 | all-reduce | flops 128 | bytes 1024 | tf_op jit(solution)/shard_map/while/body/eval_jaxpr/psum | solution.py:13
  1080.0 17.2 %psum.28 = f32[4,32]{1,0:T(4,128)S(1)} all-reduce(f32[4,32]{1,0:T(4,128)S(1)} %multiply_reduce_fusion.11), channel_id=1, replica_groups=mesh['group'=4,'expert'=8] {'expert'}, use_global_device_ids=true, to_apply=%region_11.0 | all-reduce | flops 128 | bytes 1024 | tf_op jit(solution)/shard_map/while/body/eval_jaxpr/psum | solution.py:13
  1103.3 19.1 %psum.28 = f32[4,32]{1,0:T(4,128)S(1)} all-reduce(f32[4,32]{1,0:T(4,128)S(1)} %multiply_reduce_fusion.11), channel_id=1, replica_groups=mesh['group'=4,'expert'=8] {'expert'}, use_global_device_ids=true, to_apply=%region_11.0 | all-reduce | flops 128 | bytes 1024 | tf_op jit(solution)/shard_map/while/body/eval_jaxpr/psum | solution.py:13
  1152.1 19.1 %psum.28 = f32[4,32]{1,0:T(4,128)S(1)} all-reduce(f32[4,32]{1,0:T(4,128)S(1)} %multiply_reduce_fusion.11), channel_id=1, replica_groups=mesh['group'=4,'expert'=8] {'expert'}, use_global_device_ids=true, to_apply=%region_11.0 | all-reduce | flops 128 | bytes 1024 | tf_op jit(solution)/shard_map/while/body/eval_jaxpr/psum | solution.py:13
  1235.5 20.1 %gather_fusion.1 = bf16[1024,4096]{1,0:T(8,128)(2,1)} fusion(bf16[1152,4096]{1,0:T(8,128)(2,1)} %reshape.162, s32[1024]{0:T(1024)S(1)} %broadcast_clamp_fusion), kind=kCustom, calls=%fused_computation.1 | custom fusion | bytes 16781312 | tf_op jit(solution)/shard_map/gather | solution.py:100
  (219 shorter events, 237.1 us)
Async XLA Ops:
  358.9 4.8 copy-start.6
  358.9 842.5 %copy-start.3 = (s32[128,8]{0,1:T(8,128)S(1)}, s32[128,8]{0,1:T(8,128)}, u32[]{:S(2)}) copy-start(s32[128,8]{0,1:T(8,128)} %param.14) | copy-start | bytes 12292
  358.9 850.1 %all-to-all-start.1 = ((bf16[32,4,9,4096]{3,1,2,0:T(4,128)(2,1)}), bf16[32,4,9,4096]{3,1,2,0:T(4,128)(2,1)}, u32[]{:S(2)}, u32[]{:S(2)}) async-start(bf16[32,4,9,4096]{3,1,2,0:T(4,128)(2,1)} %copy.80), calls=%async_computation.1 | async-start | bytes 18874368 | tf_op jit(solution)/shard_map/all_to_all | solution.py:91
  365.2 229.4 %copy-start.4 = (f32[128]{0:T(128)}, f32[128]{0:T(128)S(1)}, u32[]{:S(2)}) copy-start(f32[128]{0:T(128)S(1)} %broadcast_divide_fusion.2) | copy-start | bytes 1540 | tf_op jit(solution)/shard_map/while
  594.7 38.5 %copy-start.4 = (f32[128]{0:T(128)}, f32[128]{0:T(128)S(1)}, u32[]{:S(2)}) copy-start(f32[128]{0:T(128)S(1)} %broadcast_divide_fusion.2) | copy-start | bytes 1540 | tf_op jit(solution)/shard_map/while
  633.3 41.6 %copy-start.4 = (f32[128]{0:T(128)}, f32[128]{0:T(128)S(1)}, u32[]{:S(2)}) copy-start(f32[128]{0:T(128)S(1)} %broadcast_divide_fusion.2) | copy-start | bytes 1540 | tf_op jit(solution)/shard_map/while
  675.1 38.5 %copy-start.4 = (f32[128]{0:T(128)}, f32[128]{0:T(128)S(1)}, u32[]{:S(2)}) copy-start(f32[128]{0:T(128)S(1)} %broadcast_divide_fusion.2) | copy-start | bytes 1540 | tf_op jit(solution)/shard_map/while
  713.7 41.6 %copy-start.4 = (f32[128]{0:T(128)}, f32[128]{0:T(128)S(1)}, u32[]{:S(2)}) copy-start(f32[128]{0:T(128)S(1)} %broadcast_divide_fusion.2) | copy-start | bytes 1540 | tf_op jit(solution)/shard_map/while
  755.4 38.6 %copy-start.4 = (f32[128]{0:T(128)}, f32[128]{0:T(128)S(1)}, u32[]{:S(2)}) copy-start(f32[128]{0:T(128)S(1)} %broadcast_divide_fusion.2) | copy-start | bytes 1540 | tf_op jit(solution)/shard_map/while
  794.1 41.6 %copy-start.4 = (f32[128]{0:T(128)}, f32[128]{0:T(128)S(1)}, u32[]{:S(2)}) copy-start(f32[128]{0:T(128)S(1)} %broadcast_divide_fusion.2) | copy-start | bytes 1540 | tf_op jit(solution)/shard_map/while
  835.8 38.6 %copy-start.4 = (f32[128]{0:T(128)}, f32[128]{0:T(128)S(1)}, u32[]{:S(2)}) copy-start(f32[128]{0:T(128)S(1)} %broadcast_divide_fusion.2) | copy-start | bytes 1540 | tf_op jit(solution)/shard_map/while
  874.6 41.5 %copy-start.4 = (f32[128]{0:T(128)}, f32[128]{0:T(128)S(1)}, u32[]{:S(2)}) copy-start(f32[128]{0:T(128)S(1)} %broadcast_divide_fusion.2) | copy-start | bytes 1540 | tf_op jit(solution)/shard_map/while
  916.2 38.7 %copy-start.4 = (f32[128]{0:T(128)}, f32[128]{0:T(128)S(1)}, u32[]{:S(2)}) copy-start(f32[128]{0:T(128)S(1)} %broadcast_divide_fusion.2) | copy-start | bytes 1540 | tf_op jit(solution)/shard_map/while
  956.1 26.3 %copy-start.1 = (f32[128,4]{1,0:T(8,128)}, f32[128,4]{1,0:T(8,128)S(1)}, u32[]{:S(2)}) copy-start(f32[128,4]{1,0:T(8,128)S(1)} %div.73) | copy-start | bytes 6148 | tf_op jit(solution)/shard_map/while
  982.7 23.0 %copy-start.1 = (f32[128,4]{1,0:T(8,128)}, f32[128,4]{1,0:T(8,128)S(1)}, u32[]{:S(2)}) copy-start(f32[128,4]{1,0:T(8,128)S(1)} %div.73) | copy-start | bytes 6148 | tf_op jit(solution)/shard_map/while
  1006.0 25.0 %copy-start.1 = (f32[128,4]{1,0:T(8,128)}, f32[128,4]{1,0:T(8,128)S(1)}, u32[]{:S(2)}) copy-start(f32[128,4]{1,0:T(8,128)S(1)} %div.73) | copy-start | bytes 6148 | tf_op jit(solution)/shard_map/while
  1031.3 23.0 %copy-start.1 = (f32[128,4]{1,0:T(8,128)}, f32[128,4]{1,0:T(8,128)S(1)}, u32[]{:S(2)}) copy-start(f32[128,4]{1,0:T(8,128)S(1)} %div.73) | copy-start | bytes 6148 | tf_op jit(solution)/shard_map/while
  1054.6 25.0 %copy-start.1 = (f32[128,4]{1,0:T(8,128)}, f32[128,4]{1,0:T(8,128)S(1)}, u32[]{:S(2)}) copy-start(f32[128,4]{1,0:T(8,128)S(1)} %div.73) | copy-start | bytes 6148 | tf_op jit(solution)/shard_map/while
  1079.8 23.1 %copy-start.1 = (f32[128,4]{1,0:T(8,128)}, f32[128,4]{1,0:T(8,128)S(1)}, u32[]{:S(2)}) copy-start(f32[128,4]{1,0:T(8,128)S(1)} %div.73) | copy-start | bytes 6148 | tf_op jit(solution)/shard_map/while
  1103.1 25.1 %copy-start.1 = (f32[128,4]{1,0:T(8,128)}, f32[128,4]{1,0:T(8,128)S(1)}, u32[]{:S(2)}) copy-start(f32[128,4]{1,0:T(8,128)S(1)} %div.73) | copy-start | bytes 6148 | tf_op jit(solution)/shard_map/while
  1128.5 23.1 %copy-start.1 = (f32[128,4]{1,0:T(8,128)}, f32[128,4]{1,0:T(8,128)S(1)}, u32[]{:S(2)}) copy-start(f32[128,4]{1,0:T(8,128)S(1)} %div.73) | copy-start | bytes 6148 | tf_op jit(solution)/shard_map/while
  1151.9 25.1 %copy-start.1 = (f32[128,4]{1,0:T(8,128)}, f32[128,4]{1,0:T(8,128)S(1)}, u32[]{:S(2)}) copy-start(f32[128,4]{1,0:T(8,128)S(1)} %div.73) | copy-start | bytes 6148 | tf_op jit(solution)/shard_map/while
  1177.3 23.1 %copy-start.1 = (f32[128,4]{1,0:T(8,128)}, f32[128,4]{1,0:T(8,128)S(1)}, u32[]{:S(2)}) copy-start(f32[128,4]{1,0:T(8,128)S(1)} %div.73) | copy-start | bytes 6148 | tf_op jit(solution)/shard_map/while
  1208.9 10.9 copy-start.5
  (3 other events, 11.4 us)
